TPU v7x, 32 devices: a whole 2x2x4 slice. The times are simulated.
32 devices in a mesh: grp: 4 (over x, core), blk: 8 (over z, y).
Axes of the slice: x: 2, y: 2, z: 4, core: 2. Of those that a mesh axis runs over, the one named last changes fastest.
Arguments:
- raw: bfloat16 [4, 4, 1024, 256], P('grp', None, 'blk'), may hold values from -6 to 6
- raw_kin: bfloat16 [4, 4, 4, 1024], P('grp', None, None, 'blk'), may hold values from -3.2 to 20, as said below
- reader: int32 [4, 1024], P('grp', 'blk'), may hold values from 0 to 3
- event_id: int32 [4, 1024], P('grp', 'blk'), may hold values from 0 to 7, never falling along the last dimension, each value on 1 to 512 neighbouring positions
- pre_gain: float32 [256], replicated, may hold values from 0.25 to 1.75
- w_query: bfloat16 [256, 256], replicated, may hold values from -2 to 2
- w_key: bfloat16 [256, 256], replicated, may hold values from -2 to 2
- w_value: bfloat16 [256, 256], replicated, may hold values from -0.375 to 0.375
- w_out: bfloat16 [256, 256], replicated, may hold values from -0.375 to 0.375
- post_gain: float32 [256], replicated, may hold values from 0.25 to 1.75
- pair_w1: float32 [4, 32], replicated, may hold values from -3 to 3
- pair_b1: float32 [32], replicated, may hold values from -4 to 4
- pair_w2: float32 [32, 8], replicated, may hold values from -1 to 1
Outputs:
- encoded: bfloat16 [4, 1024, 256], P('grp', 'blk')
Inputs may be any that keep to these rules, and one draw needn't show every extreme that they name: `raw_kin`: rows are transverse momentum (positive), rapidity, azimuth and mass (positive). `event_id`: event numbers never fall along a group's slots; every event holds 1 to 512 slots and some event exactly 512.
All inputs are finite; a program needn't handle non-finite values.
Results may differ from a plain program's by a relative error of at most 0.0091.
Values may be sent and summed in bfloat16 or wider, within the bound.
No kernel may reach another device: no remote copies, remote signals or barrier semaphores. Data moves between devices by JAX's collectives and lax.ppermute only.
A program may use at most 64 MiB of HBM per device.

v0:
```python
import math

import jax
import jax.numpy as jnp
from jax import lax
from jax.experimental import pallas as pl
from jax.experimental.pallas import tpu as pltpu
from jax.sharding import PartitionSpec as P


F32 = jnp.float32
BF16 = jnp.bfloat16
EXTRA = 16
LANES = 128
SPAN = 32
MIB = 1 << 20

SQ = math.sqrt(2.0 / math.pi)
GAMMA = (SQ * 0.044715) ** (1.0 / 3.0)
BETA = SQ / GAMMA
LOG2E = math.log2(math.e)
LN2 = math.log(2.0)


def iota(shape, axis):
    return lax.broadcasted_iota(jnp.int32, shape, axis)


def layer_norm(rows, gain):
    center = rows - jnp.mean(rows, axis=-1, keepdims=True)
    spread = jnp.mean(center * center, axis=-1, keepdims=True)
    return center * lax.rsqrt(spread + 1e-05) * gain


def pack_kernel(raw_ref, kin_ref, reader_ref, ids_ref, pre_ref, post_ref, *refs):
    groups, rows, width = raw_ref.shape
    messages = refs[:groups]
    copies = refs[groups : groups + 4]
    kin_own, sems = refs[groups + 4 :]
    own = lax.axis_index("grp")
    moves = [
        pltpu.make_async_copy(raw_ref.at[lax.rem(own + step, groups)], out.at[pl.ds(0, rows)], sems.at[step])
        for step, out in enumerate(messages)
    ]
    first = pltpu.make_async_copy(kin_ref, kin_own, sems.at[groups])
    first.start()
    for move in moves:
        move.start()
    others = [
        pltpu.make_async_copy(source, out, sems.at[groups + 1 + at])
        for at, (source, out) in enumerate(zip((reader_ref, ids_ref, pre_ref, post_ref), copies))
    ]
    for move in others:
        move.start()
    first.wait()
    for step, out in enumerate(messages):
        kin = kin_own[lax.rem(own + step, groups)]
        out[rows : rows + EXTRA, :] = jnp.concatenate(
            [
                jnp.concatenate([kin, jnp.zeros((4, width - rows), BF16)], axis=1),
                jnp.zeros((EXTRA - 4, width), BF16),
            ],
            axis=0,
        )
    for move in moves + others:
        move.wait()


def choose_kernel(reader_ref, ids_ref, gain_ref, ready_ref, *refs):
    got = refs[:-1]
    out = refs[-1]
    groups = len(got)
    rows = got[0].shape[0] - EXTRA
    width = got[0].shape[1]
    own = lax.axis_index("grp")
    by_lane = reader_ref[...].astype(F32)
    by_row = jnp.transpose(jnp.broadcast_to(by_lane, (LANES, rows)))
    by_row = jnp.concatenate([by_row] * (width // LANES), axis=1)
    tokens = jnp.zeros((rows, width), F32)
    kin = jnp.zeros((4, rows), F32)
    for step, ref in enumerate(got):
        source = lax.rem(own + groups - step, groups).astype(F32)
        tokens = jnp.where(by_row == source, ref[0:rows, :].astype(F32), tokens)
        kin = jnp.where(by_lane == source, ref[rows : rows + EXTRA, 0:rows].astype(F32)[0:4], kin)
    out[0:rows, :] = layer_norm(tokens, gain_ref[...]).astype(BF16)
    block = jnp.concatenate([kin, ids_ref[...].astype(F32), jnp.zeros((EXTRA - 5, rows), F32)], axis=0)
    block = jnp.concatenate([block, jnp.zeros((EXTRA, width - rows), F32)], axis=1)
    out[rows : rows + EXTRA, :] = block.astype(BF16)


def split(value):
    high = value.astype(BF16)
    return high, (value - high.astype(F32)).astype(BF16)


def weights_kernel(*refs):
    sources = refs[:7]
    copies = refs[7:11]
    first_ref, second_ref, w1_ref, b1_ref, w2_ref, sems = refs[11:]
    moves = [
        pltpu.make_async_copy(source, out, sems.at[at])
        for at, (source, out) in enumerate(zip(sources, (w1_ref, b1_ref, w2_ref, *copies)))
    ]
    for move in moves:
        move.start()
    for move in moves[:3]:
        move.wait()
    hidden = w1_ref.shape[1]
    heads = w2_ref.shape[0]
    row = lax.broadcasted_iota(jnp.int32, (4, hidden), 0)
    w1 = w1_ref[...] * jnp.where(row == 2, GAMMA, GAMMA * LN2)
    w1_hi, w1_lo = split(w1)
    b1 = b1_ref[...] * GAMMA
    b_hi, b_mid = split(b1)
    b_lo = b1 - b_hi.astype(F32) - b_mid.astype(F32)
    stack = jnp.concatenate(
        [
            w1_hi.astype(F32),
            w1_lo.astype(F32),
            b_hi.astype(F32),
            b_mid.astype(F32),
            b_lo,
            jnp.zeros((5, hidden), F32),
        ],
        axis=0,
    ).astype(BF16)

    def onehot(hit):
        return jnp.where(hit, 1.0, 0.0).astype(BF16)

    units = hidden * 8
    grown = onehot(iota((hidden, units), 1) // 8 == iota((hidden, units), 0))
    tall = jnp.dot(stack, grown, preferred_element_type=F32).astype(BF16)
    col = iota((16, LANES), 1)
    which = jnp.where(col < 32, col // 8, jnp.where(col < 96, col // 8 - 4, col - 88))
    pick = onehot((which == iota((16, LANES), 0)) & (col < 99))
    first = lax.dot_general(tall, pick, (((0,), (0,)), ((), ())), preferred_element_type=F32)
    col = iota((units, LANES), 1)
    same = (iota((units, LANES), 0) % 8 == col % 8) | (col >= 96)
    first_ref[...] = jnp.where(same, first, 0.0).astype(BF16)

    w2_hi, w2_lo = split(w2_ref[...] * (LOG2E * 0.5 / GAMMA))
    wide = [jnp.dot(w, grown, preferred_element_type=F32) for w in (w2_hi, w2_lo)]
    wide = jnp.concatenate(wide, axis=0).astype(BF16)
    shape = (16 * heads, 2 * heads)
    lift = onehot(iota(shape, 0) // 8 == iota(shape, 1))
    second = jnp.dot(lift, wide, preferred_element_type=F32)
    shape = (16 * heads, units)
    second_ref[...] = jnp.where(iota(shape, 0) % 8 == iota(shape, 1) % 8, second, 0.0).astype(BF16)
    for move in moves[3:]:
        move.wait()


def key_side(got, checks, wk_ref, wv_ref, x_ref, k_ref, v_ref, raw_ref, term_ref):
    count = len(got)
    rows = got[0].shape[0] - EXTRA
    width = got[0].shape[1]
    for place, (ref, check) in enumerate(zip(got, checks)):
        x_ref[place] = ref[0:rows, :]
        extra = ref[rows : rows + EXTRA, 0:rows].astype(F32)
        for row in range(4):
            raw_ref[row, place : place + 1, :] = extra[row : row + 1, :]
        event = extra[4:5, :]
        raw_ref[4, place : place + 1, :] = event if check is None else jnp.where(check, event, -1.0)
    feats = x_ref[...].reshape(count * rows, width)
    shape = (count, rows, width)
    k_ref[...] = jnp.dot(feats, wk_ref[...], preferred_element_type=F32).astype(BF16).reshape(shape)
    v_ref[...] = jnp.dot(feats, wv_ref[...], preferred_element_type=F32).astype(BF16).reshape(shape)
    pt = raw_ref[0]
    rap = raw_ref[1]
    phi = raw_ref[2]
    mass = raw_ref[3]
    m2 = mass * mass
    mt = jnp.sqrt(pt * pt + m2)
    terms = (pt, rap, jnp.cos(phi), jnp.sin(phi), mt * jnp.exp(rap), mt * jnp.exp(-rap), m2, raw_ref[4])
    for t, term in enumerate(terms):
        term_ref[t] = term


def query_side(mine_ref, wq_ref, term_ref, qt_ref, qm_ref, heads):
    rows = mine_ref.shape[0] - EXTRA
    width = mine_ref.shape[1]
    groups = SPAN // 8
    lines = 8 * heads
    mine = jnp.concatenate([term_ref[t, 0:1, :] for t in range(8)], axis=0)
    factor = iota((8, rows), 0)
    scaled = jnp.where((factor == 2) | (factor == 3), mine * 2.0, mine)
    scaled = jnp.where(factor == 6, mine + 1.0, scaled)
    cols = jnp.transpose(jnp.concatenate([scaled, jnp.zeros((LANES - 8, rows), F32)], axis=0))
    for t in range(8):
        qt_ref[t] = jnp.broadcast_to(cols[:, t : t + 1], (rows, LANES))
    queries = jnp.dot(mine_ref[0:rows, :], wq_ref[...], preferred_element_type=F32).astype(BF16).astype(F32)
    lane_head = iota((8, width), 1) // (width // heads)
    for g in range(rows // 8):
        piece = queries[8 * g : 8 * g + 8, :]
        qm_ref[g // groups, (g % groups) * lines : (g % groups + 1) * lines, :] = jnp.concatenate(
            [jnp.where(lane_head == h, piece, 0.0) for h in range(heads)], axis=0
        ).astype(BF16)


def pair_scores(
    mine_ref, first_ref, second_ref, qt_ref, qm_ref, k_ref, term_ref, f_ref, act_ref, s_ref, table_ref, heads
):
    blocks, rows, width = k_ref.shape
    spans = rows // SPAN
    groups = SPAN // 8
    lines = 8 * heads
    scale = LOG2E * (width // heads) ** (-0.5)

    ids = term_ref[7]
    least = jnp.min(ids, axis=1, keepdims=True)
    most = jnp.max(ids, axis=1, keepdims=True)
    weight = jnp.left_shift(1, iota((blocks, 1), 0)).astype(F32)
    q_ids = mine_ref[rows : rows + EXTRA, 0:rows].astype(F32)[4:5, :]
    lane = iota((1, rows), 1) // SPAN
    count = jnp.int32(0)
    for s in range(spans):
        q_least = jnp.min(jnp.where(lane == s, q_ids, 1e9), axis=1, keepdims=True)
        q_most = jnp.max(jnp.where(lane == s, q_ids, -1e9), axis=1, keepdims=True)
        live = (least <= q_most) & (most >= q_least)
        bits = jnp.sum(jnp.where(live, weight, 0.0)).astype(jnp.int32)
        for place in range(blocks):
            bit = lax.bitwise_and(lax.shift_right_logical(bits, place), 1)
            table_ref[count] = jnp.int32(16 * s + place)
            count = count + bit

            @pl.when(bit == 0)
            def blank(place=place, s=s):
                s_ref[place, s] = jnp.full((SPAN * heads, LANES), -1e30, F32)

    f_ref[96:128, :] = jnp.ones((32, groups * LANES), BF16)

    def features(s, j):
        k = [term_ref[t, pl.ds(j, 1), :] for t in range(7)]
        for g in range(groups):
            at = pl.multiple_of(s * SPAN + 8 * g, 8)
            q = [qt_ref[t, pl.ds(at, 8), :] for t in range(7)]
            gap = q[1] - k[1]
            cos_gap = q[2] * k[2] + q[3] * k[3]
            dist = gap * gap + (2.0 - cos_gap)
            low = jnp.minimum(q[0], k[0])
            pair_mass = (q[6] + k[6]) + (q[4] * k[5] + q[5] * k[4] - (q[0] * k[0]) * cos_gap)
            ab = jnp.concatenate([jnp.log2(1.0 + dist), jnp.log2(1.0 + low * low * dist)], axis=0)
            cd = jnp.concatenate([low / (q[0] + k[0]), jnp.log2(pair_mass)], axis=0)
            ab_hi, ab_lo = split(ab)
            cd_hi, cd_lo = split(cd)
            f_ref[0:96, g * LANES : (g + 1) * LANES] = jnp.concatenate(
                [ab_hi, cd_hi, ab_lo, cd_lo, ab_hi, cd_hi], axis=0
            )

    def score(s, j):
        bias2 = jnp.dot(second_ref[...], act_ref[...], preferred_element_type=F32)
        bias = bias2[0:lines, :] + bias2[lines:, :]
        match = lax.dot_general(
            qm_ref[s], k_ref[j], (((1,), (1,)), ((), ())), preferred_element_type=F32
        )
        key_ids = term_ref[7, pl.ds(j, 1), :]
        for g in range(groups):
            at = pl.multiple_of(s * SPAN + 8 * g, 8)
            live = qt_ref[7, pl.ds(at, 8), :] == key_ids
            for h in range(heads):
                line = g * lines + 8 * h
                value = match[line : line + 8, :] * scale + bias[8 * h : 8 * h + 8, g * LANES : (g + 1) * LANES]
                s_ref[j, s, line : line + 8, :] = jnp.where(live, value, -1e30)

    def task(at):
        code = table_ref[jnp.clip(at, 0, count - 1)]
        return lax.shift_right_logical(code, 4), lax.bitwise_and(code, 15)

    def step(at, carry):
        hidden = jnp.dot(first_ref[...], f_ref[...], preferred_element_type=F32)
        features(*task(at + 1))
        score(*task(at - 1))
        act = hidden * (1.0 + jnp.tanh(hidden * (hidden * hidden + BETA)))
        act_ref[...] = act.astype(BF16)
        return carry

    @pl.when(count > 0)
    def run():
        features(*task(0))
        lax.fori_loop(0, count, step, 0)
        score(*task(count - 1))


def own_kernel(mine_ref, wq_ref, wk_ref, wv_ref, first_ref, second_ref, s_ref, v_ref, qt_ref, qm_ref, *scratch, heads):
    x_ref, k_ref, raw_ref, term_ref, f_ref, act_ref, table_ref = scratch
    key_side([mine_ref], [None], wk_ref, wv_ref, x_ref, k_ref, v_ref, raw_ref, term_ref)
    query_side(mine_ref, wq_ref, term_ref, qt_ref, qm_ref, heads)
    pair_scores(
        mine_ref, first_ref, second_ref, qt_ref, qm_ref, k_ref, term_ref, f_ref, act_ref, s_ref, table_ref, heads
    )


def reaches(place, flip, blocks):
    return abs(place - (place ^ flip)) <= blocks // 2


def useful(flip, blocks):
    if not skips(flip, blocks):
        return None
    own = lax.axis_index("blk")
    return jnp.abs(own - lax.bitwise_xor(own, flip)) <= blocks // 2


def skips(flip, blocks):
    return blocks == 8 and not all(reaches(place, flip, blocks) for place in range(blocks))


def near_kernel(mine_ref, *refs, flips, blocks, heads):
    count = len(flips)
    got = refs[:count]
    wk_ref, wv_ref, first_ref, second_ref, qt_ref, qm_ref, s_ref, v_ref = refs[count : count + 8]
    x_ref, k_ref, raw_ref, term_ref, f_ref, act_ref, table_ref = refs[count + 8 :]
    checks = [useful(flip, blocks) for flip in flips]
    key_side(got, checks, wk_ref, wv_ref, x_ref, k_ref, v_ref, raw_ref, term_ref)
    pair_scores(
        mine_ref, first_ref, second_ref, qt_ref, qm_ref, k_ref, term_ref, f_ref, act_ref, s_ref, table_ref, heads
    )


def last_kernel(mine_ref, *refs, flips, blocks, heads):
    count = len(flips)
    got = refs[:count]
    wk_ref, wv_ref, first_ref, second_ref, qt_ref, qm_ref = refs[count : count + 6]
    s_own, s_near, v_own, v_near, wo_ref, gain_ref, out_ref = refs[count + 6 : count + 13]
    x_ref, k_ref, raw_ref, term_ref, f_ref, act_ref, table_ref, s_ref, v_ref, att_ref = refs[count + 13 :]
    checks = [useful(flip, blocks) for flip in flips]
    key_side(got, checks, wk_ref, wv_ref, x_ref, k_ref, v_ref, raw_ref, term_ref)
    pair_scores(
        mine_ref, first_ref, second_ref, qt_ref, qm_ref, k_ref, term_ref, f_ref, act_ref, s_ref, table_ref, heads
    )
    rows = out_ref.shape[0]
    width = out_ref.shape[1]
    lines = 8 * heads
    deep = (SPAN * heads, width)
    diag = (iota(deep, 0) % lines) // 8 == iota(deep, 1) // (width // heads)
    parts = [(s_own, v_own), (s_near, v_near), (s_ref, v_ref)]

    def attend(s, carry):
        top = None
        for scores, _ in parts:
            for j in range(scores.shape[0]):
                top = scores[j, s] if top is None else jnp.maximum(top, scores[j, s])
        top = jnp.max(top, axis=1, keepdims=True)
        total = jnp.zeros((SPAN * heads, LANES), F32)
        accum = jnp.zeros(deep, F32)
        for scores, values in parts:
            pieces = []
            for j in range(scores.shape[0]):
                weights = jnp.exp2(scores[j, s] - top)
                total = total + weights
                pieces.append(weights.astype(BF16))
            accum = accum + jnp.dot(
                jnp.concatenate(pieces, axis=1),
                values[...].reshape(len(pieces) * rows, width),
                preferred_element_type=F32,
            )
        total = jnp.sum(total, axis=1, keepdims=True)
        accum = jnp.where(diag, accum / total, 0.0)
        for g in range(SPAN // 8):
            out = accum[g * lines : g * lines + 8, :]
            for h in range(1, heads):
                out = out + accum[g * lines + 8 * h : g * lines + 8 * h + 8, :]
            att_ref[pl.ds(pl.multiple_of(s * SPAN + 8 * g, 8), 8), :] = out
        return carry

    lax.fori_loop(0, rows // SPAN, attend, 0)
    mixed = jnp.dot(att_ref[...].astype(BF16), wo_ref[...], preferred_element_type=F32)
    out_ref[...] = layer_norm(mixed, gain_ref[...]).astype(BF16)


def shards(
    raw,
    raw_kin,
    reader,
    event_id,
    pre_gain,
    w_query,
    w_key,
    w_value,
    w_out,
    post_gain,
    pair_w1,
    pair_b1,
    pair_w2,
):
    groups = raw.shape[1]
    rows = raw.shape[2]
    width = raw.shape[3]
    blocks = lax.axis_size("blk")
    heads = pair_w2.shape[1]
    hidden = pair_w1.shape[1]
    assert rows == LANES and blocks & (blocks - 1) == 0 and blocks <= 32
    raw = raw[0]
    raw_kin = raw_kin[0]
    array = jax.ShapeDtypeStruct
    message = array((rows + EXTRA, width), BF16)
    vmem = pl.BlockSpec(memory_space=pltpu.VMEM)
    hbm = pl.BlockSpec(memory_space=pltpu.HBM)

    def call(kernel, out_shape, operands, scratch=(), limit=8, specs=None):
        single = not isinstance(out_shape, list)
        return pl.pallas_call(
            kernel,
            out_shape=out_shape,
            in_specs=specs or [vmem] * len(operands),
            out_specs=vmem if single else [vmem] * len(out_shape),
            scratch_shapes=list(scratch),
            compiler_params=pltpu.CompilerParams(vmem_limit_bytes=limit * MIB),
        )(*[pltpu.with_memory_space_constraint(a, pltpu.HBM) for a in operands] if specs else operands)

    small = [reader, event_id, pre_gain[None], post_gain[None]]
    packed = call(
        pack_kernel,
        [message] * groups + [array(a.shape, a.dtype) for a in small],
        [raw, raw_kin, *small],
        [pltpu.VMEM(raw_kin.shape, BF16), pltpu.SemaphoreType.DMA((groups + 5,))],
        specs=[hbm] * 6,
    )
    reader, event_id, pre_row, post_row = packed[groups:]
    parts = [packed[0]] + [
        lax.ppermute(packed[s], "grp", [(i, (i + s) % groups) for i in range(groups)])
        for s in range(1, groups)
    ]
    local = [pair_w1, pair_b1[None], pair_w2.T]
    dense = [w_query, w_key, w_value, w_out]
    w_query, w_key, w_value, w_out, first, second = call(
        weights_kernel,
        [array(a.shape, a.dtype) for a in dense]
        + [array((8 * hidden, LANES), BF16), array((16 * heads, 8 * hidden), BF16)],
        local + dense,
        [pltpu.VMEM(a.shape, a.dtype) for a in local] + [pltpu.SemaphoreType.DMA((7,))],
        specs=[hbm] * 7,
    )
    mine = call(choose_kernel, message, [reader, event_id, pre_row, first, *parts])

    along = [4, 2, 6] if blocks == 8 else list(range(2, blocks, 2))
    soon = along[:2] + [1] + along[2:]
    late = [flip ^ 1 for flip in (2, 6, 4)] if blocks == 8 else [flip ^ 1 for flip in along]

    def swap(part, flip):
        pairs = [(i, i ^ flip) for i in range(blocks)]
        if flip in along and skips(flip, blocks):
            pairs = [(i, i ^ flip if reaches(i, flip, blocks) else i ^ 1) for i in range(blocks)]
        return lax.ppermute(part, "blk", pairs)

    messages = {flip: swap(mine, flip) for flip in (soon if blocks == 8 else soon[:2])}

    spans = rows // SPAN
    lanes = SPAN // 8 * LANES
    tall = SPAN * heads

    def scratch(count):
        return [
            pltpu.VMEM((count, rows, width), BF16),
            pltpu.VMEM((count, rows, width), BF16),
            pltpu.VMEM((5, count, rows), F32),
            pltpu.VMEM((8, count, rows), F32),
            pltpu.VMEM((LANES, lanes), BF16),
            pltpu.VMEM((8 * hidden, lanes), BF16),
            pltpu.SMEM((spans * count + 1,), jnp.int32),
        ]

    def results(count):
        return [array((count, spans, tall, LANES), F32), array((count, rows, width), BF16)]

    s_own, v_own, q_terms, q_heads = call(
        lambda *refs: own_kernel(*refs, heads=heads),
        results(1) + [array((8, rows, LANES), F32), array((spans, tall, width), BF16)],
        [mine, w_query, w_key, w_value, first, second],
        scratch(1),
        limit=10,
    )
    held, q_terms = lax.optimization_barrier((mine, q_terms))
    messages.update({flip: swap(held, flip) for flip in soon if flip not in messages})
    messages.update({flip: swap(messages[flip ^ 1], 1) for flip in late})
    s_near, v_near = call(
        lambda *refs: near_kernel(*refs, flips=soon, blocks=blocks, heads=heads),
        results(len(soon)),
        [mine, *[messages[flip] for flip in soon], w_key, w_value, first, second, q_terms, q_heads],
        scratch(len(soon)),
        limit=12 + blocks // 2,
    )
    far_scratch = scratch(len(late))
    far_shapes = [
        pltpu.VMEM((len(late), spans, tall, LANES), F32),
        pltpu.VMEM((len(late), rows, width), BF16),
        pltpu.VMEM((rows, width), F32),
    ]
    encoded = call(
        lambda *refs: last_kernel(*refs, flips=late, blocks=blocks, heads=heads),
        array((rows, width), BF16),
        [mine, *[messages[flip] for flip in late], w_key, w_value, first, second, q_terms, q_heads]
        + [s_own, s_near, v_own, v_near, w_out, post_row],
        far_scratch + far_shapes,
        limit=14 + 3 * blocks // 2,
    )
    return encoded[None]


def solution(mesh):
    in_specs = (
        P("grp", None, "blk", None),
        P("grp", None, None, "blk"),
        P("grp", "blk"),
        P("grp", "blk"),
        P(),
        P(),
        P(),
        P(),
        P(),
        P(),
        P(),
        P(),
        P(),
    )
    out_specs = P("grp", "blk", None)

    return jax.shard_map(shards, mesh=mesh, in_specs=in_specs, out_specs=out_specs, check_vma=False)
```

profile of v0, /device:TPU:26, one launch (start us, length us, event | category | flops | bytes accessed | tf_op | source)
XLA Modules:
  0.0 30.1 jit_solution(18386593366462337190)
XLA Ops:
  0.0 1.0 %shard_map.127 = (bf16[144,256]{1,0:T(8,128)(2,1)S(1)}, bf16[144,256]{1,0:T(8,128)(2,1)S(1)}, bf16[144,256]{1,0:T(8,128)(2,1)S(1)}, bf16[144,256]{1,0:T(8,128)(2...) custom-call(bf16[4,128,256]{2,1,0:T(8,128)(2,1)} %bitcast.7, ...), custom_call_target="tpu_custom_call" | custom-call | tf_op jit(solution)/shard_map/pallas_call | solution.py:403
  1.0 0.1 collective-permute-start
  1.1 0.6 %collective-permute-start.1 = (bf16[144,256]{1,0:T(8,128)(2,1)S(1)}, bf16[144,256]{1,0:T(8,128)(2,1)S(1)}, u32[]{:S(2)}, u32[]{:S(2)}) collective-permute-start(bf16[144,256]{1,0:T(8,128)(2,1)S(1)} %get-tuple-element.32), channel_id=1, source_target_pairs={{0,16},{8,24},{16,0},{24,8},{1,17},{9,25},{17,1},{25,9},{2,18},{10... | collective-permute-start | bytes 221192 | tf_op jit(solution)/shard_map/ppermute | solution.py:422
  1.7 1.4 %collective-permute-start.2 = (bf16[144,256]{1,0:T(8,128)(2,1)S(1)}, bf16[144,256]{1,0:T(8,128)(2,1)S(1)}, u32[]{:S(2)}, u32[]{:S(2)}) collective-permute-start(bf16[144,256]{1,0:T(8,128)(2,1)S(1)} %get-tuple-element.33), channel_id=1, source_target_pairs={{0,24},{8,0},{16,8},{24,16},{1,25},{9,1},{17,9},{25,17},{2,26},{10... | collective-permute-start | bytes 221192 | tf_op jit(solution)/shard_map/ppermute | solution.py:422
  3.1 1.2 %shard_map.128 = (bf16[256,256]{1,0:T(8,128)(2,1)S(1)}, bf16[256,256]{1,0:T(8,128)(2,1)S(1)}, bf16[256,256]{1,0:T(8,128)(2,1)S(1)}, bf16[256,256]{1,0:T(8,128)(2...) custom-call(f32[4,32]{1,0:T(4,128)} %refs_0_.1, f32[1,32]{1,0:T(1,128)} %bitcast.12, ...), custom_call_target="tpu_custom_call" | custom-call | tf_op jit(solution)/shard_map/pallas_call | solution.py:403
  4.3 0.7 %collective-permute-done.refs_1_ = bf16[144,256]{1,0:T(8,128)(2,1)S(1)} collective-permute-done((bf16[144,256]{1,0:T(8,128)(2,1)S(1)}, bf16[144,256]{1,0:T(8,128)(2,1)S(1)}, u32[]{:S(2)}, u32[]{:S(2)}) %collective-permute-start) | collective-permute-done | bytes 73760 | tf_op jit(solution)/shard_map/ppermute | solution.py:422
  5.0 1.3 %collective-permute-done.1.refs_2_ = bf16[144,256]{1,0:T(8,128)(2,1)S(1)} collective-permute-done((bf16[144,256]{1,0:T(8,128)(2,1)S(1)}, bf16[144,256]{1,0:T(8,128)(2,1)S(1)}, u32[]{:S(2)}, u32[]{:S(2)}) %collective-permute-start.1) | collective-permute-done | bytes 73760 | tf_op jit(solution)/shard_map/ppermute | solution.py:422
  6.3 0.0 collective-permute-done.2.refs_3_
  6.3 0.3 shard_map.129.refs_0_
  6.6 0.5 %collective-permute-start.3 = (bf16[144,256]{1,0:T(8,128)(2,1)S(1)}, bf16[144,256]{1,0:T(8,128)(2,1)S(1)}, u32[]{:S(2)}, u32[]{:S(2)}) collective-permute-start(bf16[144,256]{1,0:T(8,128)(2,1)S(1)} %shard_map.129.refs_0_), channel_id=1, source_target_pairs={{0,2},{1,3},{2,0},{3,1},{4,6},{5,7},{6,4},{7,5},{8,10},{9,11},{10,... | collective-permute-start | bytes 221192 | tf_op jit(solution)/shard_map/ppermute | solution.py:445
  7.1 1.5 %collective-permute-start.5 = (bf16[144,256]{1,0:T(8,128)(2,1)S(1)}, bf16[144,256]{1,0:T(8,128)(2,1)S(1)}, u32[]{:S(2)}, u32[]{:S(2)}) collective-permute-start(bf16[144,256]{1,0:T(8,128)(2,1)S(1)} %shard_map.129.refs_0_), channel_id=1, source_target_pairs={{0,1},{1,0},{2,4},{3,5},{4,2},{5,3},{6,7},{7,6},{8,9},{9,8},{10,12... | collective-permute-start | bytes 221192 | tf_op jit(solution)/shard_map/ppermute | solution.py:445
  8.6 1.5 %collective-permute-start.7 = (bf16[144,256]{1,0:T(8,128)(2,1)S(1)}, bf16[144,256]{1,0:T(8,128)(2,1)S(1)}, u32[]{:S(2)}, u32[]{:S(2)}) collective-permute-start(bf16[144,256]{1,0:T(8,128)(2,1)S(1)} %shard_map.129.refs_0_), channel_id=1, source_target_pairs={{0,4},{1,5},{2,6},{3,7},{4,0},{5,1},{6,2},{7,3},{8,12},{9,13},{10,... | collective-permute-start | bytes 221192 | tf_op jit(solution)/shard_map/ppermute | solution.py:445
  10.2 1.5 %collective-permute-start.9 = (bf16[144,256]{1,0:T(8,128)(2,1)S(1)}, bf16[144,256]{1,0:T(8,128)(2,1)S(1)}, u32[]{:S(2)}, u32[]{:S(2)}) collective-permute-start(bf16[144,256]{1,0:T(8,128)(2,1)S(1)} %shard_map.129.refs_0_), channel_id=1, source_target_pairs={{0,1},{1,0},{2,3},{3,2},{4,5},{5,4},{6,7},{7,6},{8,9},{9,8},{10,11... | collective-permute-start | bytes 221192 | tf_op jit(solution)/shard_map/ppermute | solution.py:445
  11.7 0.0 collective-permute-done.3.refs_2_
  11.7 1.4 %collective-permute-start.4 = (bf16[144,256]{1,0:T(8,128)(2,1)S(1)}, bf16[144,256]{1,0:T(8,128)(2,1)S(1)}, u32[]{:S(2)}, u32[]{:S(2)}) collective-permute-start(bf16[144,256]{1,0:T(8,128)(2,1)S(1)} %collective-permute-done.3.refs_2_), channel_id=1, source_target_pairs={{0,1},{1,0},{2,3},{3,2},{4,5},{5,4},{6,7},{7,6},{8,9},{9,8},{10,11... | collective-permute-start | bytes 221192 | tf_op jit(solution)/shard_map/ppermute | solution.py:445
  13.1 0.0 collective-permute-done.5.refs_4_
  13.1 0.6 %collective-permute-start.6 = (bf16[144,256]{1,0:T(8,128)(2,1)S(1)}, bf16[144,256]{1,0:T(8,128)(2,1)S(1)}, u32[]{:S(2)}, u32[]{:S(2)}) collective-permute-start(bf16[144,256]{1,0:T(8,128)(2,1)S(1)} %collective-permute-done.5.refs_4_), channel_id=1, source_target_pairs={{0,1},{1,0},{2,3},{3,2},{4,5},{5,4},{6,7},{7,6},{8,9},{9,8},{10,11... | collective-permute-start | bytes 221192 | tf_op jit(solution)/shard_map/ppermute | solution.py:445
  13.7 2.2 %collective-permute-done.7.refs_1_ = bf16[144,256]{1,0:T(8,128)(2,1)S(1)} collective-permute-done((bf16[144,256]{1,0:T(8,128)(2,1)S(1)}, bf16[144,256]{1,0:T(8,128)(2,1)S(1)}, u32[]{:S(2)}, u32[]{:S(2)}) %collective-permute-start.7) | collective-permute-done | bytes 73760 | tf_op jit(solution)/shard_map/ppermute | solution.py:445
  15.9 1.5 %collective-permute-start.8 = (bf16[144,256]{1,0:T(8,128)(2,1)S(1)}, bf16[144,256]{1,0:T(8,128)(2,1)S(1)}, u32[]{:S(2)}, u32[]{:S(2)}) collective-permute-start(bf16[144,256]{1,0:T(8,128)(2,1)S(1)} %collective-permute-done.7.refs_1_), channel_id=1, source_target_pairs={{0,1},{1,0},{2,3},{3,2},{4,5},{5,4},{6,7},{7,6},{8,9},{9,8},{10,11... | collective-permute-start | bytes 221192 | tf_op jit(solution)/shard_map/ppermute | solution.py:445
  17.5 2.3 %shard_map.130 = (f32[1,4,256,128]{3,2,1,0:T(8,128)S(1)}, bf16[1,128,256]{2,1,0:T(8,128)(2,1)S(1)}, f32[8,128,128]{2,1,0:T(8,128)S(1)}, bf16[4,256,256]{2,1,0:T(8,128)(2,1)S(1)}) custom-call(bf16[144,256]{1,0:T(8,128)(2,1)S(1)} %shard_map.129.refs_0_, bf16[256,256]{1,0:T(8,128)(2,1)S(1)} %get-tuple-element.37.refs_1_, ...), custom_call_target="tpu_custom_call" | custom-call | tf_op jit(solution)/shard_map/pallas_call | solution.py:403
  19.8 0.0 collective-permute-done.9.refs_3_
  19.8 3.8 %shard_map.131 = (f32[4,4,256,128]{3,2,1,0:T(8,128)S(1)}, bf16[4,128,256]{2,1,0:T(8,128)(2,1)S(1)}) custom-call(bf16[144,256]{1,0:T(8,128)(2,1)S(1)} %shard_map.129.refs_0_, bf16[144,256]{1,0:T(8,128)(2,1)S(1)} %collective-permute-done.7.refs_1_, bf16[144,256]{1,0:T(8,128)(2,1)S(1)} %collective-permute-done.3.refs_2_, ...), custom_call_target="tpu_custom_call" | custom-call | tf_op jit(solution)/shard_map/pallas_call | solution.py:403
  23.5 0.0 collective-permute-done.4.refs_1_
  23.6 0.0 collective-permute-done.6.refs_2_
  23.6 0.0 collective-permute-done.8.refs_3_
  23.6 6.6 %shard_map.132 = bf16[128,256]{1,0:T(8,128)(2,1)} custom-call(bf16[144,256]{1,0:T(8,128)(2,1)S(1)} %shard_map.129.refs_0_, bf16[144,256]{1,0:T(8,128)(2,1)S(1)} %collective-permute-done.4.refs_1_, bf16[144,256]{1,0:T(8,128)(2,1)S(1)} %collective-permute-done.6.refs_2_, bf16[144,256]{1,0:T(8,128)(2,1)S(1)} %collective-permute-done.8.refs_3_, ...), custom_call_target="tpu_custom_call" | custom-call | tf_op jit(solution)/shard_map/pallas_call | solution.py:403
Async XLA Ops:
  1.0 4.0 %collective-permute-start = (bf16[144,256]{1,0:T(8,128)(2,1)S(1)}, bf16[144,256]{1,0:T(8,128)(2,1)S(1)}, u32[]{:S(2)}, u32[]{:S(2)}) collective-permute-start(bf16[144,256]{1,0:T(8,128)(2,1)S(1)} %get-tuple-element.31), channel_id=1, source_target_pairs={{0,8},{8,16},{16,24},{24,0},{1,9},{9,17},{17,25},{25,1},{2,10},{10... | collective-permute-start | bytes 221192 | tf_op jit(solution)/shard_map/ppermute | solution.py:422
  1.1 5.2 %collective-permute-start.1 = (bf16[144,256]{1,0:T(8,128)(2,1)S(1)}, bf16[144,256]{1,0:T(8,128)(2,1)S(1)}, u32[]{:S(2)}, u32[]{:S(2)}) collective-permute-start(bf16[144,256]{1,0:T(8,128)(2,1)S(1)} %get-tuple-element.32), channel_id=1, source_target_pairs={{0,16},{8,24},{16,0},{24,8},{1,17},{9,25},{17,1},{25,9},{2,18},{10... | collective-permute-start | bytes 221192 | tf_op jit(solution)/shard_map/ppermute | solution.py:422
  1.7 4.6 %collective-permute-start.2 = (bf16[144,256]{1,0:T(8,128)(2,1)S(1)}, bf16[144,256]{1,0:T(8,128)(2,1)S(1)}, u32[]{:S(2)}, u32[]{:S(2)}) collective-permute-start(bf16[144,256]{1,0:T(8,128)(2,1)S(1)} %get-tuple-element.33), channel_id=1, source_target_pairs={{0,24},{8,0},{16,8},{24,16},{1,25},{9,1},{17,9},{25,17},{2,26},{10... | collective-permute-start | bytes 221192 | tf_op jit(solution)/shard_map/ppermute | solution.py:422
  6.6 5.1 %collective-permute-start.3 = (bf16[144,256]{1,0:T(8,128)(2,1)S(1)}, bf16[144,256]{1,0:T(8,128)(2,1)S(1)}, u32[]{:S(2)}, u32[]{:S(2)}) collective-permute-start(bf16[144,256]{1,0:T(8,128)(2,1)S(1)} %shard_map.129.refs_0_), channel_id=1, source_target_pairs={{0,2},{1,3},{2,0},{3,1},{4,6},{5,7},{6,4},{7,5},{8,10},{9,11},{10,... | collective-permute-start | bytes 221192 | tf_op jit(solution)/shard_map/ppermute | solution.py:445
  7.1 6.0 %collective-permute-start.5 = (bf16[144,256]{1,0:T(8,128)(2,1)S(1)}, bf16[144,256]{1,0:T(8,128)(2,1)S(1)}, u32[]{:S(2)}, u32[]{:S(2)}) collective-permute-start(bf16[144,256]{1,0:T(8,128)(2,1)S(1)} %shard_map.129.refs_0_), channel_id=1, source_target_pairs={{0,1},{1,0},{2,4},{3,5},{4,2},{5,3},{6,7},{7,6},{8,9},{9,8},{10,12... | collective-permute-start | bytes 221192 | tf_op jit(solution)/shard_map/ppermute | solution.py:445
  8.6 7.3 %collective-permute-start.7 = (bf16[144,256]{1,0:T(8,128)(2,1)S(1)}, bf16[144,256]{1,0:T(8,128)(2,1)S(1)}, u32[]{:S(2)}, u32[]{:S(2)}) collective-permute-start(bf16[144,256]{1,0:T(8,128)(2,1)S(1)} %shard_map.129.refs_0_), channel_id=1, source_target_pairs={{0,4},{1,5},{2,6},{3,7},{4,0},{5,1},{6,2},{7,3},{8,12},{9,13},{10,... | collective-permute-start | bytes 221192 | tf_op jit(solution)/shard_map/ppermute | solution.py:445
  10.2 9.6 %collective-permute-start.9 = (bf16[144,256]{1,0:T(8,128)(2,1)S(1)}, bf16[144,256]{1,0:T(8,128)(2,1)S(1)}, u32[]{:S(2)}, u32[]{:S(2)}) collective-permute-start(bf16[144,256]{1,0:T(8,128)(2,1)S(1)} %shard_map.129.refs_0_), channel_id=1, source_target_pairs={{0,1},{1,0},{2,3},{3,2},{4,5},{5,4},{6,7},{7,6},{8,9},{9,8},{10,11... | collective-permute-start | bytes 221192 | tf_op jit(solution)/shard_map/ppermute | solution.py:445
  11.7 11.9 %collective-permute-start.4 = (bf16[144,256]{1,0:T(8,128)(2,1)S(1)}, bf16[144,256]{1,0:T(8,128)(2,1)S(1)}, u32[]{:S(2)}, u32[]{:S(2)}) collective-permute-start(bf16[144,256]{1,0:T(8,128)(2,1)S(1)} %collective-permute-done.3.refs_2_), channel_id=1, source_target_pairs={{0,1},{1,0},{2,3},{3,2},{4,5},{5,4},{6,7},{7,6},{8,9},{9,8},{10,11... | collective-permute-start | bytes 221192 | tf_op jit(solution)/shard_map/ppermute | solution.py:445
  13.1 10.5 %collective-permute-start.6 = (bf16[144,256]{1,0:T(8,128)(2,1)S(1)}, bf16[144,256]{1,0:T(8,128)(2,1)S(1)}, u32[]{:S(2)}, u32[]{:S(2)}) collective-permute-start(bf16[144,256]{1,0:T(8,128)(2,1)S(1)} %collective-permute-done.5.refs_4_), channel_id=1, source_target_pairs={{0,1},{1,0},{2,3},{3,2},{4,5},{5,4},{6,7},{7,6},{8,9},{9,8},{10,11... | collective-permute-start | bytes 221192 | tf_op jit(solution)/shard_map/ppermute | solution.py:445
  15.9 7.6 %collective-permute-start.8 = (bf16[144,256]{1,0:T(8,128)(2,1)S(1)}, bf16[144,256]{1,0:T(8,128)(2,1)S(1)}, u32[]{:S(2)}, u32[]{:S(2)}) collective-permute-start(bf16[144,256]{1,0:T(8,128)(2,1)S(1)} %collective-permute-done.7.refs_1_), channel_id=1, source_target_pairs={{0,1},{1,0},{2,3},{3,2},{4,5},{5,4},{6,7},{7,6},{8,9},{9,8},{10,11... | collective-permute-start | bytes 221192 | tf_op jit(solution)/shard_map/ppermute | solution.py:445
where the time goes:
time: 30.3 us; the launch traced here: 30.1 us
  Pallas kernels  15.1 us (50%)
  starting transfers between devices  10.7 us (35%)
  waiting for transfers between devices  4.24 us (14%)
    pallas_call x6, Pallas kernels, call(): pl.pallas_call(kernel, out_shape=out_shape, in_specs=specs or [vmem] * le...  15.1 us
    ppermute x7, starting transfers between devices, swap(): return lax.ppermute(part, 'blk', pairs)  8.62 us
    ppermute x7, waiting for transfers between devices, swap(): return lax.ppermute(part, 'blk', pairs)  2.23 us
    ppermute x3, starting transfers between devices, shards(): lax.ppermute(packed[s], 'grp', [(i, (i + s) % groups) for i in range(grou...  2.05 us
    ppermute x3, waiting for transfers between devices, shards(): lax.ppermute(packed[s], 'grp', [(i, (i + s) % groups) for i in range(grou...  2.01 us
  transfers between devices with their start and end apart: 10, of which 3 were waited for; matrix products, arithmetic and copies ran while one was open for 0% of the time, Pallas kernels for 24%

commit v1 on v0

--- a/solution.py
+++ b/solution.py
@@ -10,7 +10,7 @@
 
 F32 = jnp.float32
 BF16 = jnp.bfloat16
-EXTRA = 16
+EXTRA = 8
 LANES = 128
 SPAN = 32
 MIB = 1 << 20
@@ -199,7 +199,7 @@
 
 
 def pair_scores(
-    mine_ref, first_ref, second_ref, qt_ref, qm_ref, k_ref, term_ref, f_ref, act_ref, s_ref, table_ref, heads
+    mine_ref, first_ref, second_ref, qt_ref, qm_ref, k_ref, term_ref, f_ref, h_ref, act_ref, s_ref, table_ref, heads
 ):
     blocks, rows, width = k_ref.shape
     spans = rows // SPAN
@@ -212,22 +212,35 @@
     most = jnp.max(ids, axis=1, keepdims=True)
     weight = jnp.left_shift(1, iota((blocks, 1), 0)).astype(F32)
     q_ids = mine_ref[rows : rows + EXTRA, 0:rows].astype(F32)[4:5, :]
-    lane = iota((1, rows), 1) // SPAN
+    inside = iota((8, rows), 1) // SPAN == iota((8, rows), 0)
+    q_least = jnp.min(jnp.where(inside, q_ids, 1e9), axis=1, keepdims=True)
+    q_most = jnp.max(jnp.where(inside, q_ids, -1e9), axis=1, keepdims=True)
+    joint = max(1, 24 // blocks)
+    codes = []
+    for base in range(0, spans, joint):
+        code = jnp.zeros((blocks, 1), F32)
+        for s in range(base, min(base + joint, spans)):
+            live = (least <= q_most[s : s + 1]) & (most >= q_least[s : s + 1])
+            code = code + jnp.where(live, weight * float(1 << (blocks * (s - base))), 0.0)
+        codes.append(jnp.sum(code).astype(jnp.int32))
     count = jnp.int32(0)
+    dead = jnp.int32(0)
     for s in range(spans):
-        q_least = jnp.min(jnp.where(lane == s, q_ids, 1e9), axis=1, keepdims=True)
-        q_most = jnp.max(jnp.where(lane == s, q_ids, -1e9), axis=1, keepdims=True)
-        live = (least <= q_most) & (most >= q_least)
-        bits = jnp.sum(jnp.where(live, weight, 0.0)).astype(jnp.int32)
         for place in range(blocks):
-            bit = lax.bitwise_and(lax.shift_right_logical(bits, place), 1)
-            table_ref[count] = jnp.int32(16 * s + place)
+            bit = lax.bitwise_and(lax.shift_right_logical(codes[s // joint], blocks * (s % joint) + place), 1)
+            table_ref[0, count] = jnp.int32(16 * s + place)
+            table_ref[1, dead] = jnp.int32(16 * s + place)
             count = count + bit
-
-            @pl.when(bit == 0)
-            def blank(place=place, s=s):
-                s_ref[place, s] = jnp.full((SPAN * heads, LANES), -1e30, F32)
-
+            dead = dead + (1 - bit)
+
+    def blank(at, carry):
+        code = table_ref[1, at]
+        s_ref[lax.bitwise_and(code, 15), lax.shift_right_logical(code, 4)] = jnp.full(
+            (SPAN * heads, LANES), -1e30, F32
+        )
+        return carry
+
+    lax.fori_loop(0, dead, blank, 0)
     f_ref[96:128, :] = jnp.ones((32, groups * LANES), BF16)
 
     def features(s, j):
@@ -264,30 +277,38 @@
                 s_ref[j, s, line : line + 8, :] = jnp.where(live, value, -1e30)
 
     def task(at):
-        code = table_ref[jnp.clip(at, 0, count - 1)]
+        code = table_ref[0, jnp.clip(at, 0, count - 1)]
         return lax.shift_right_logical(code, 4), lax.bitwise_and(code, 15)
 
+    half = groups * LANES // 2
+
+    def activate(hidden):
+        return (hidden * (1.0 + jnp.tanh(hidden * (hidden * hidden + BETA)))).astype(BF16)
+
     def step(at, carry):
-        hidden = jnp.dot(first_ref[...], f_ref[...], preferred_element_type=F32)
+        left = jnp.dot(first_ref[...], f_ref[:, 0:half], preferred_element_type=F32)
+        right = jnp.dot(first_ref[...], f_ref[:, half:], preferred_element_type=F32)
+        act_ref[:, half:] = activate(h_ref[...])
         features(*task(at + 1))
         score(*task(at - 1))
-        act = hidden * (1.0 + jnp.tanh(hidden * (hidden * hidden + BETA)))
-        act_ref[...] = act.astype(BF16)
+        h_ref[...] = right
+        act_ref[:, 0:half] = activate(left)
         return carry
 
     @pl.when(count > 0)
     def run():
         features(*task(0))
         lax.fori_loop(0, count, step, 0)
+        act_ref[:, half:] = activate(h_ref[...])
         score(*task(count - 1))
 
 
 def own_kernel(mine_ref, wq_ref, wk_ref, wv_ref, first_ref, second_ref, s_ref, v_ref, qt_ref, qm_ref, *scratch, heads):
-    x_ref, k_ref, raw_ref, term_ref, f_ref, act_ref, table_ref = scratch
+    x_ref, k_ref, raw_ref, term_ref, f_ref, h_ref, act_ref, table_ref = scratch
     key_side([mine_ref], [None], wk_ref, wv_ref, x_ref, k_ref, v_ref, raw_ref, term_ref)
     query_side(mine_ref, wq_ref, term_ref, qt_ref, qm_ref, heads)
     pair_scores(
-        mine_ref, first_ref, second_ref, qt_ref, qm_ref, k_ref, term_ref, f_ref, act_ref, s_ref, table_ref, heads
+        mine_ref, first_ref, second_ref, qt_ref, qm_ref, k_ref, term_ref, f_ref, h_ref, act_ref, s_ref, table_ref, heads
     )
 
 
@@ -310,11 +331,11 @@
     count = len(flips)
     got = refs[:count]
     wk_ref, wv_ref, first_ref, second_ref, qt_ref, qm_ref, s_ref, v_ref = refs[count : count + 8]
-    x_ref, k_ref, raw_ref, term_ref, f_ref, act_ref, table_ref = refs[count + 8 :]
+    x_ref, k_ref, raw_ref, term_ref, f_ref, h_ref, act_ref, table_ref = refs[count + 8 :]
     checks = [useful(flip, blocks) for flip in flips]
     key_side(got, checks, wk_ref, wv_ref, x_ref, k_ref, v_ref, raw_ref, term_ref)
     pair_scores(
-        mine_ref, first_ref, second_ref, qt_ref, qm_ref, k_ref, term_ref, f_ref, act_ref, s_ref, table_ref, heads
+        mine_ref, first_ref, second_ref, qt_ref, qm_ref, k_ref, term_ref, f_ref, h_ref, act_ref, s_ref, table_ref, heads
     )
 
 
@@ -323,11 +344,11 @@
     got = refs[:count]
     wk_ref, wv_ref, first_ref, second_ref, qt_ref, qm_ref = refs[count : count + 6]
     s_own, s_near, v_own, v_near, wo_ref, gain_ref, out_ref = refs[count + 6 : count + 13]
-    x_ref, k_ref, raw_ref, term_ref, f_ref, act_ref, table_ref, s_ref, v_ref, att_ref = refs[count + 13 :]
+    x_ref, k_ref, raw_ref, term_ref, f_ref, h_ref, act_ref, table_ref, s_ref, v_ref, att_ref, top_ref = refs[count + 13 :]
     checks = [useful(flip, blocks) for flip in flips]
     key_side(got, checks, wk_ref, wv_ref, x_ref, k_ref, v_ref, raw_ref, term_ref)
     pair_scores(
-        mine_ref, first_ref, second_ref, qt_ref, qm_ref, k_ref, term_ref, f_ref, act_ref, s_ref, table_ref, heads
+        mine_ref, first_ref, second_ref, qt_ref, qm_ref, k_ref, term_ref, f_ref, h_ref, act_ref, s_ref, table_ref, heads
     )
     rows = out_ref.shape[0]
     width = out_ref.shape[1]
@@ -336,12 +357,15 @@
     diag = (iota(deep, 0) % lines) // 8 == iota(deep, 1) // (width // heads)
     parts = [(s_own, v_own), (s_near, v_near), (s_ref, v_ref)]
 
-    def attend(s, carry):
+    def largest(s):
         top = None
         for scores, _ in parts:
             for j in range(scores.shape[0]):
                 top = scores[j, s] if top is None else jnp.maximum(top, scores[j, s])
-        top = jnp.max(top, axis=1, keepdims=True)
+        top_ref[s] = jnp.broadcast_to(jnp.max(top, axis=1, keepdims=True), (SPAN * heads, LANES))
+
+    def attend(s, carry):
+        top = top_ref[s]
         total = jnp.zeros((SPAN * heads, LANES), F32)
         accum = jnp.zeros(deep, F32)
         for scores, values in parts:
@@ -355,8 +379,9 @@
                 values[...].reshape(len(pieces) * rows, width),
                 preferred_element_type=F32,
             )
-        total = jnp.sum(total, axis=1, keepdims=True)
-        accum = jnp.where(diag, accum / total, 0.0)
+        largest(jnp.minimum(s + 1, rows // SPAN - 1))
+        inverse = 1.0 / jnp.sum(total, axis=1, keepdims=True)
+        accum = jnp.where(diag, accum * inverse, 0.0)
         for g in range(SPAN // 8):
             out = accum[g * lines : g * lines + 8, :]
             for h in range(1, heads):
@@ -364,6 +389,7 @@
             att_ref[pl.ds(pl.multiple_of(s * SPAN + 8 * g, 8), 8), :] = out
         return carry
 
+    largest(0)
     lax.fori_loop(0, rows // SPAN, attend, 0)
     mixed = jnp.dot(att_ref[...].astype(BF16), wo_ref[...], preferred_element_type=F32)
     out_ref[...] = layer_norm(mixed, gain_ref[...]).astype(BF16)
@@ -457,8 +483,9 @@
             pltpu.VMEM((5, count, rows), F32),
             pltpu.VMEM((8, count, rows), F32),
             pltpu.VMEM((LANES, lanes), BF16),
+            pltpu.VMEM((8 * hidden, lanes // 2), F32),
             pltpu.VMEM((8 * hidden, lanes), BF16),
-            pltpu.SMEM((spans * count + 1,), jnp.int32),
+            pltpu.SMEM((2, spans * count + 1), jnp.int32),
         ]
 
     def results(count):
@@ -486,6 +513,7 @@
         pltpu.VMEM((len(late), spans, tall, LANES), F32),
         pltpu.VMEM((len(late), rows, width), BF16),
         pltpu.VMEM((rows, width), F32),
+        pltpu.VMEM((spans, tall, LANES), F32),
     ]
     encoded = call(
         lambda *refs: last_kernel(*refs, flips=late, blocks=blocks, heads=heads),

time: 30.3 us -> 28.3 us (0.934)
  Pallas kernels: 15.1 us -> 13.5 us
  waiting for transfers between devices: 4.24 us -> 3.81 us
    pallas_call x6, Pallas kernels: 15.1 us -> 13.5 us  [call(): pl.pallas_call(kernel, out_shape=out_shape, in_specs=specs or [vmem] * le...]
    ppermute x7, waiting for transfers between devices: 2.23 us -> 1.88 us  [swap(): return lax.ppermute(part, 'blk', pairs)]
  transfers between devices with their start and end apart: 10 -> 10, of which waited for: 3 -> 3; matrix products, arithmetic and copies ran while one was open for 0% -> 0% of each run, Pallas kernels for 24% -> 23%
where the time goes in v1:
time: 28.3 us; the launch traced here: 28.1 us
  Pallas kernels  13.5 us (48%)
  starting transfers between devices  10.7 us (38%)
  waiting for transfers between devices  3.81 us (13%)
    pallas_call x6, Pallas kernels, call(): pl.pallas_call(kernel, out_shape=out_shape, in_specs=specs or [vmem] * le...  13.5 us
    ppermute x7, starting transfers between devices, swap(): return lax.ppermute(part, 'blk', pairs)  8.62 us
    ppermute x3, starting transfers between devices, shards(): lax.ppermute(packed[s], 'grp', [(i, (i + s) % groups) for i in range(grou...  2.05 us
    ppermute x3, waiting for transfers between devices, shards(): lax.ppermute(packed[s], 'grp', [(i, (i + s) % groups) for i in range(grou...  1.93 us
    ppermute x7, waiting for transfers between devices, swap(): return lax.ppermute(part, 'blk', pairs)  1.88 us
  transfers between devices with their start and end apart: 10, of which 3 were waited for; matrix products, arithmetic and copies ran while one was open for 0% of the time, Pallas kernels for 23%

profile of v1, /device:TPU:26, one launch (start us, length us, event | category | flops | bytes accessed | tf_op | source)
XLA Modules:
  0.0 28.1 jit_solution(10023840927551179791)
XLA Ops:
  0.0 1.0 %shard_map.127 = (bf16[136,256]{1,0:T(8,128)(2,1)S(1)}, bf16[136,256]{1,0:T(8,128)(2,1)S(1)}, bf16[136,256]{1,0:T(8,128)(2,1)S(1)}, bf16[136,256]{1,0:T(8,128)(2...) custom-call(bf16[4,128,256]{2,1,0:T(8,128)(2,1)} %bitcast.7, ...), custom_call_target="tpu_custom_call" | custom-call | tf_op jit(solution)/shard_map/pallas_call | solution.py:429
  1.0 0.1 collective-permute-start
  1.1 0.6 %collective-permute-start.1 = (bf16[136,256]{1,0:T(8,128)(2,1)S(1)}, bf16[136,256]{1,0:T(8,128)(2,1)S(1)}, u32[]{:S(2)}, u32[]{:S(2)}) collective-permute-start(bf16[136,256]{1,0:T(8,128)(2,1)S(1)} %get-tuple-element.32), channel_id=1, source_target_pairs={{0,16},{8,24},{16,0},{24,8},{1,17},{9,25},{17,1},{25,9},{2,18},{10... | collective-permute-start | bytes 208904 | tf_op jit(solution)/shard_map/ppermute | solution.py:448
  1.7 1.4 %collective-permute-start.2 = (bf16[136,256]{1,0:T(8,128)(2,1)S(1)}, bf16[136,256]{1,0:T(8,128)(2,1)S(1)}, u32[]{:S(2)}, u32[]{:S(2)}) collective-permute-start(bf16[136,256]{1,0:T(8,128)(2,1)S(1)} %get-tuple-element.33), channel_id=1, source_target_pairs={{0,24},{8,0},{16,8},{24,16},{1,25},{9,1},{17,9},{25,17},{2,26},{10... | collective-permute-start | bytes 208904 | tf_op jit(solution)/shard_map/ppermute | solution.py:448
  3.1 1.2 %shard_map.128 = (bf16[256,256]{1,0:T(8,128)(2,1)S(1)}, bf16[256,256]{1,0:T(8,128)(2,1)S(1)}, bf16[256,256]{1,0:T(8,128)(2,1)S(1)}, bf16[256,256]{1,0:T(8,128)(2...) custom-call(f32[4,32]{1,0:T(4,128)} %refs_0_.1, f32[1,32]{1,0:T(1,128)} %bitcast.12, ...), custom_call_target="tpu_custom_call" | custom-call | tf_op jit(solution)/shard_map/pallas_call | solution.py:429
  4.3 0.6 %collective-permute-done.refs_1_ = bf16[136,256]{1,0:T(8,128)(2,1)S(1)} collective-permute-done((bf16[136,256]{1,0:T(8,128)(2,1)S(1)}, bf16[136,256]{1,0:T(8,128)(2,1)S(1)}, u32[]{:S(2)}, u32[]{:S(2)}) %collective-permute-start) | collective-permute-done | bytes 69664 | tf_op jit(solution)/shard_map/ppermute | solution.py:448
  4.9 1.3 %collective-permute-done.1.refs_2_ = bf16[136,256]{1,0:T(8,128)(2,1)S(1)} collective-permute-done((bf16[136,256]{1,0:T(8,128)(2,1)S(1)}, bf16[136,256]{1,0:T(8,128)(2,1)S(1)}, u32[]{:S(2)}, u32[]{:S(2)}) %collective-permute-start.1) | collective-permute-done | bytes 69664 | tf_op jit(solution)/shard_map/ppermute | solution.py:448
  6.2 0.0 collective-permute-done.2.refs_3_
  6.2 0.3 shard_map.129.refs_0_
  6.5 0.5 %collective-permute-start.3 = (bf16[136,256]{1,0:T(8,128)(2,1)S(1)}, bf16[136,256]{1,0:T(8,128)(2,1)S(1)}, u32[]{:S(2)}, u32[]{:S(2)}) collective-permute-start(bf16[136,256]{1,0:T(8,128)(2,1)S(1)} %shard_map.129.refs_0_), channel_id=1, source_target_pairs={{0,2},{1,3},{2,0},{3,1},{4,6},{5,7},{6,4},{7,5},{8,10},{9,11},{10,... | collective-permute-start | bytes 208904 | tf_op jit(solution)/shard_map/ppermute | solution.py:471
  7.0 1.5 %collective-permute-start.5 = (bf16[136,256]{1,0:T(8,128)(2,1)S(1)}, bf16[136,256]{1,0:T(8,128)(2,1)S(1)}, u32[]{:S(2)}, u32[]{:S(2)}) collective-permute-start(bf16[136,256]{1,0:T(8,128)(2,1)S(1)} %shard_map.129.refs_0_), channel_id=1, source_target_pairs={{0,1},{1,0},{2,4},{3,5},{4,2},{5,3},{6,7},{7,6},{8,9},{9,8},{10,12... | collective-permute-start | bytes 208904 | tf_op jit(solution)/shard_map/ppermute | solution.py:471
  8.6 1.5 %collective-permute-start.7 = (bf16[136,256]{1,0:T(8,128)(2,1)S(1)}, bf16[136,256]{1,0:T(8,128)(2,1)S(1)}, u32[]{:S(2)}, u32[]{:S(2)}) collective-permute-start(bf16[136,256]{1,0:T(8,128)(2,1)S(1)} %shard_map.129.refs_0_), channel_id=1, source_target_pairs={{0,4},{1,5},{2,6},{3,7},{4,0},{5,1},{6,2},{7,3},{8,12},{9,13},{10,... | collective-permute-start | bytes 208904 | tf_op jit(solution)/shard_map/ppermute | solution.py:471
  10.1 1.5 %collective-permute-start.9 = (bf16[136,256]{1,0:T(8,128)(2,1)S(1)}, bf16[136,256]{1,0:T(8,128)(2,1)S(1)}, u32[]{:S(2)}, u32[]{:S(2)}) collective-permute-start(bf16[136,256]{1,0:T(8,128)(2,1)S(1)} %shard_map.129.refs_0_), channel_id=1, source_target_pairs={{0,1},{1,0},{2,3},{3,2},{4,5},{5,4},{6,7},{7,6},{8,9},{9,8},{10,11... | collective-permute-start | bytes 208904 | tf_op jit(solution)/shard_map/ppermute | solution.py:471
  11.6 0.0 collective-permute-done.3.refs_2_
  11.6 1.2 %collective-permute-start.4 = (bf16[136,256]{1,0:T(8,128)(2,1)S(1)}, bf16[136,256]{1,0:T(8,128)(2,1)S(1)}, u32[]{:S(2)}, u32[]{:S(2)}) collective-permute-start(bf16[136,256]{1,0:T(8,128)(2,1)S(1)} %collective-permute-done.3.refs_2_), channel_id=1, source_target_pairs={{0,1},{1,0},{2,3},{3,2},{4,5},{5,4},{6,7},{7,6},{8,9},{9,8},{10,11... | collective-permute-start | bytes 208904 | tf_op jit(solution)/shard_map/ppermute | solution.py:471
  12.8 0.0 collective-permute-done.5.refs_4_
  12.8 0.8 %collective-permute-start.6 = (bf16[136,256]{1,0:T(8,128)(2,1)S(1)}, bf16[136,256]{1,0:T(8,128)(2,1)S(1)}, u32[]{:S(2)}, u32[]{:S(2)}) collective-permute-start(bf16[136,256]{1,0:T(8,128)(2,1)S(1)} %collective-permute-done.5.refs_4_), channel_id=1, source_target_pairs={{0,1},{1,0},{2,3},{3,2},{4,5},{5,4},{6,7},{7,6},{8,9},{9,8},{10,11... | collective-permute-start | bytes 208904 | tf_op jit(solution)/shard_map/ppermute | solution.py:471
  13.6 1.9 %collective-permute-done.7.refs_1_ = bf16[136,256]{1,0:T(8,128)(2,1)S(1)} collective-permute-done((bf16[136,256]{1,0:T(8,128)(2,1)S(1)}, bf16[136,256]{1,0:T(8,128)(2,1)S(1)}, u32[]{:S(2)}, u32[]{:S(2)}) %collective-permute-start.7) | collective-permute-done | bytes 69664 | tf_op jit(solution)/shard_map/ppermute | solution.py:471
  15.5 1.5 %collective-permute-start.8 = (bf16[136,256]{1,0:T(8,128)(2,1)S(1)}, bf16[136,256]{1,0:T(8,128)(2,1)S(1)}, u32[]{:S(2)}, u32[]{:S(2)}) collective-permute-start(bf16[136,256]{1,0:T(8,128)(2,1)S(1)} %collective-permute-done.7.refs_1_), channel_id=1, source_target_pairs={{0,1},{1,0},{2,3},{3,2},{4,5},{5,4},{6,7},{7,6},{8,9},{9,8},{10,11... | collective-permute-start | bytes 208904 | tf_op jit(solution)/shard_map/ppermute | solution.py:471
  17.0 2.0 %shard_map.130 = (f32[1,4,256,128]{3,2,1,0:T(8,128)S(1)}, bf16[1,128,256]{2,1,0:T(8,128)(2,1)S(1)}, f32[8,128,128]{2,1,0:T(8,128)S(1)}, bf16[4,256,256]{2,1,0:T(8,128)(2,1)S(1)}) custom-call(bf16[136,256]{1,0:T(8,128)(2,1)S(1)} %shard_map.129.refs_0_, bf16[256,256]{1,0:T(8,128)(2,1)S(1)} %get-tuple-element.37.refs_1_, ...), custom_call_target="tpu_custom_call" | custom-call | tf_op jit(solution)/shard_map/pallas_call | solution.py:429
  19.0 0.0 collective-permute-done.9.refs_3_
  19.0 3.2 %shard_map.131 = (f32[4,4,256,128]{3,2,1,0:T(8,128)S(1)}, bf16[4,128,256]{2,1,0:T(8,128)(2,1)S(1)}) custom-call(bf16[136,256]{1,0:T(8,128)(2,1)S(1)} %shard_map.129.refs_0_, bf16[136,256]{1,0:T(8,128)(2,1)S(1)} %collective-permute-done.7.refs_1_, bf16[136,256]{1,0:T(8,128)(2,1)S(1)} %collective-permute-done.3.refs_2_, ...), custom_call_target="tpu_custom_call" | custom-call | tf_op jit(solution)/shard_map/pallas_call | solution.py:429
  22.2 0.0 collective-permute-done.4.refs_1_
  22.2 0.0 collective-permute-done.6.refs_2_
  22.2 0.0 collective-permute-done.8.refs_3_
  22.2 5.9 %shard_map.132 = bf16[128,256]{1,0:T(8,128)(2,1)} custom-call(bf16[136,256]{1,0:T(8,128)(2,1)S(1)} %shard_map.129.refs_0_, bf16[136,256]{1,0:T(8,128)(2,1)S(1)} %collective-permute-done.4.refs_1_, bf16[136,256]{1,0:T(8,128)(2,1)S(1)} %collective-permute-done.6.refs_2_, bf16[136,256]{1,0:T(8,128)(2,1)S(1)} %collective-permute-done.8.refs_3_, ...), custom_call_target="tpu_custom_call" | custom-call | tf_op jit(solution)/shard_map/pallas_call | solution.py:429
Async XLA Ops:
  1.0 3.9 %collective-permute-start = (bf16[136,256]{1,0:T(8,128)(2,1)S(1)}, bf16[136,256]{1,0:T(8,128)(2,1)S(1)}, u32[]{:S(2)}, u32[]{:S(2)}) collective-permute-start(bf16[136,256]{1,0:T(8,128)(2,1)S(1)} %get-tuple-element.31), channel_id=1, source_target_pairs={{0,8},{8,16},{16,24},{24,0},{1,9},{9,17},{17,25},{25,1},{2,10},{10... | collective-permute-start | bytes 208904 | tf_op jit(solution)/shard_map/ppermute | solution.py:448
  1.1 5.1 %collective-permute-start.1 = (bf16[136,256]{1,0:T(8,128)(2,1)S(1)}, bf16[136,256]{1,0:T(8,128)(2,1)S(1)}, u32[]{:S(2)}, u32[]{:S(2)}) collective-permute-start(bf16[136,256]{1,0:T(8,128)(2,1)S(1)} %get-tuple-element.32), channel_id=1, source_target_pairs={{0,16},{8,24},{16,0},{24,8},{1,17},{9,25},{17,1},{25,9},{2,18},{10... | collective-permute-start | bytes 208904 | tf_op jit(solution)/shard_map/ppermute | solution.py:448
  1.7 4.5 %collective-permute-start.2 = (bf16[136,256]{1,0:T(8,128)(2,1)S(1)}, bf16[136,256]{1,0:T(8,128)(2,1)S(1)}, u32[]{:S(2)}, u32[]{:S(2)}) collective-permute-start(bf16[136,256]{1,0:T(8,128)(2,1)S(1)} %get-tuple-element.33), channel_id=1, source_target_pairs={{0,24},{8,0},{16,8},{24,16},{1,25},{9,1},{17,9},{25,17},{2,26},{10... | collective-permute-start | bytes 208904 | tf_op jit(solution)/shard_map/ppermute | solution.py:448
  6.5 5.1 %collective-permute-start.3 = (bf16[136,256]{1,0:T(8,128)(2,1)S(1)}, bf16[136,256]{1,0:T(8,128)(2,1)S(1)}, u32[]{:S(2)}, u32[]{:S(2)}) collective-permute-start(bf16[136,256]{1,0:T(8,128)(2,1)S(1)} %shard_map.129.refs_0_), channel_id=1, source_target_pairs={{0,2},{1,3},{2,0},{3,1},{4,6},{5,7},{6,4},{7,5},{8,10},{9,11},{10,... | collective-permute-start | bytes 208904 | tf_op jit(solution)/shard_map/ppermute | solution.py:471
  7.0 5.8 %collective-permute-start.5 = (bf16[136,256]{1,0:T(8,128)(2,1)S(1)}, bf16[136,256]{1,0:T(8,128)(2,1)S(1)}, u32[]{:S(2)}, u32[]{:S(2)}) collective-permute-start(bf16[136,256]{1,0:T(8,128)(2,1)S(1)} %shard_map.129.refs_0_), channel_id=1, source_target_pairs={{0,1},{1,0},{2,4},{3,5},{4,2},{5,3},{6,7},{7,6},{8,9},{9,8},{10,12... | collective-permute-start | bytes 208904 | tf_op jit(solution)/shard_map/ppermute | solution.py:471
  8.6 6.9 %collective-permute-start.7 = (bf16[136,256]{1,0:T(8,128)(2,1)S(1)}, bf16[136,256]{1,0:T(8,128)(2,1)S(1)}, u32[]{:S(2)}, u32[]{:S(2)}) collective-permute-start(bf16[136,256]{1,0:T(8,128)(2,1)S(1)} %shard_map.129.refs_0_), channel_id=1, source_target_pairs={{0,4},{1,5},{2,6},{3,7},{4,0},{5,1},{6,2},{7,3},{8,12},{9,13},{10,... | collective-permute-start | bytes 208904 | tf_op jit(solution)/shard_map/ppermute | solution.py:471
  10.1 8.9 %collective-permute-start.9 = (bf16[136,256]{1,0:T(8,128)(2,1)S(1)}, bf16[136,256]{1,0:T(8,128)(2,1)S(1)}, u32[]{:S(2)}, u32[]{:S(2)}) collective-permute-start(bf16[136,256]{1,0:T(8,128)(2,1)S(1)} %shard_map.129.refs_0_), channel_id=1, source_target_pairs={{0,1},{1,0},{2,3},{3,2},{4,5},{5,4},{6,7},{7,6},{8,9},{9,8},{10,11... | collective-permute-start | bytes 208904 | tf_op jit(solution)/shard_map/ppermute | solution.py:471
  11.6 10.6 %collective-permute-start.4 = (bf16[136,256]{1,0:T(8,128)(2,1)S(1)}, bf16[136,256]{1,0:T(8,128)(2,1)S(1)}, u32[]{:S(2)}, u32[]{:S(2)}) collective-permute-start(bf16[136,256]{1,0:T(8,128)(2,1)S(1)} %collective-permute-done.3.refs_2_), channel_id=1, source_target_pairs={{0,1},{1,0},{2,3},{3,2},{4,5},{5,4},{6,7},{7,6},{8,9},{9,8},{10,11... | collective-permute-start | bytes 208904 | tf_op jit(solution)/shard_map/ppermute | solution.py:471
  12.8 9.3 %collective-permute-start.6 = (bf16[136,256]{1,0:T(8,128)(2,1)S(1)}, bf16[136,256]{1,0:T(8,128)(2,1)S(1)}, u32[]{:S(2)}, u32[]{:S(2)}) collective-permute-start(bf16[136,256]{1,0:T(8,128)(2,1)S(1)} %collective-permute-done.5.refs_4_), channel_id=1, source_target_pairs={{0,1},{1,0},{2,3},{3,2},{4,5},{5,4},{6,7},{7,6},{8,9},{9,8},{10,11... | collective-permute-start | bytes 208904 | tf_op jit(solution)/shard_map/ppermute | solution.py:471
  15.5 6.7 %collective-permute-start.8 = (bf16[136,256]{1,0:T(8,128)(2,1)S(1)}, bf16[136,256]{1,0:T(8,128)(2,1)S(1)}, u32[]{:S(2)}, u32[]{:S(2)}) collective-permute-start(bf16[136,256]{1,0:T(8,128)(2,1)S(1)} %collective-permute-done.7.refs_1_), channel_id=1, source_target_pairs={{0,1},{1,0},{2,3},{3,2},{4,5},{5,4},{6,7},{7,6},{8,9},{9,8},{10,11... | collective-permute-start | bytes 208904 | tf_op jit(solution)/shard_map/ppermute | solution.py:471
